TPU v7x, 256 devices: a whole 4x4x8 slice. The times are simulated.
256 devices in a mesh: seq: 32 (over x_hi, z, core), ch: 8 (over y, x_lo).
Axes of the slice: x: 4 (x_hi: 2, x_lo: 2; x = x_hi * 2 + x_lo), y: 4, z: 8, core: 2. Of those that a mesh axis runs over, the one named last changes fastest.
Arguments:
- hidden: bfloat16 [4096, 2048], P('seq', 'ch'), may hold values from -400 to 400, as said below
- tokens: int32 [4096], replicated, may hold values from 0 to 3
- edit_bounds: int32 [8, 2], replicated, may hold values from 0 to 4095
- norm_gain: float32 [2048], replicated, may hold values from 0.1 to 1.9
- base_embed: float32 [4, 2048], replicated, may hold values from -6 to 6
- w_in: bfloat16 [2, 2048, 4096], P(None, None, 'ch'), may hold values from -0.125 to 0.125
- conv_w: float32 [4, 4096], P(None, 'ch'), may hold values from -3 to 3
- conv_b: float32 [4096], P('ch'), may hold values from -3 to 3
- proj_bc: bfloat16 [32, 4096], P(None, 'ch'), may hold values from -0.1875 to 0.1875
- decay_rate: float32 [16, 4096], P(None, 'ch'), may hold values from 9.765625e-06 to 0.11, as said below
- skip_gain: float32 [4096], P('ch'), may hold values from -4 to 4
- w_out: bfloat16 [4096, 2048], P('ch'), may hold values from -0.09375 to 0.09375
Outputs:
- mixed: bfloat16 [4096, 2048], P('seq', 'ch')
Inputs may be any that keep to these rules, and one draw needn't show every extreme that they name: The hidden states have row and column scales that differ. `decay_rate`: each entry is a positive decay rate per position. `edit_bounds`: positions in the window; a span's start and end come in no fixed order and may coincide with others.
All inputs are finite; a program needn't handle non-finite values.
Results may differ from a plain program's by a relative error of at most 0.014.
Values may be sent and summed in bfloat16 or wider, within the bound.
A program may use at most 64 MiB of HBM per device.

v0:
```python
import jax
import jax.numpy as jnp
from jax import lax
from jax.sharding import PartitionSpec as P

CONV = 4
epsilon = 1e-05


def from_partner(block, axis, apart):
    count = lax.axis_size(axis)
    route = []
    for low in range(count):
        high = low | 1 << apart
        if high != low and high < count:
            route += [(low, high), (high, low)]
    return lax.ppermute(block, axis, route)


def passed_along(block, axis, distance):
    devices = range(lax.axis_size(axis))
    route = [(i - distance, i) for i in devices if i - distance in devices]
    return lax.ppermute(block, axis, route)


def carried_in(part, axis, combine, identity):
    place = lax.axis_index(axis)
    gathered = jax.tree.map(lambda a: lax.all_gather(a, axis), part)
    state = jax.tree.map(lambda a, e: jnp.zeros_like(a) + jnp.asarray(e, a.dtype), part, identity)

    def one(step, state):
        return combine(
            state, jax.tree.map(lambda a: lax.dynamic_index_in_dim(a, step, 0, False), gathered)
        )

    return lax.fori_loop(0, place, one, state)


def link(before, follow):
    return (before[0] * follow[0], before[1] * follow[0] + follow[1])


def link_pair(before, follow):
    return link(before[0:2], follow[0:2]) + link(before[2:4], follow[2:4])


def keep_rows(places, edit_bounds):
    hit_count = jnp.sum(
        (places[:, None] == edit_bounds.reshape(-1)[None, :]).astype(jnp.float32), axis=1
    )
    return 1.0 / (1.0 + hit_count)


def norm_rows(rows, bases, norm_gain, base_embed):
    row_values = rows.astype(jnp.float32)
    inv_rms = lax.rsqrt(jnp.mean(row_values * row_values, axis=1, keepdims=True) + epsilon)
    one_hot = (bases[:, None] == jnp.arange(4, dtype=jnp.int32)[None, :]).astype(jnp.float32)
    embedded = one_hot[:, 0:1] * base_embed[0][None, :]
    for base_index in range(1, 4):
        embedded = (
            embedded + one_hot[:, base_index : base_index + 1] * base_embed[base_index][None, :]
        )
    return (row_values * inv_rms * norm_gain[None, :] + embedded).astype(jnp.bfloat16)


def run_chain(
    start_state, keep_both, inputs_b, inputs_r, mixed_both, decay_mult, drive_gain, want_rows
):
    row_count = mixed_both.shape[1]
    inner_width = mixed_both.shape[2]
    state_size = inputs_b.shape[1]
    turns = 8
    per_turn = row_count // turns
    keep_blocks = keep_both.T.reshape(turns, per_turn, 2)
    b_blocks = inputs_b.transpose(2, 0, 1).reshape(turns, per_turn, 2, state_size)
    r_blocks = inputs_r.transpose(2, 0, 1).reshape(turns, per_turn, 2, state_size)
    x_blocks = mixed_both.transpose(1, 0, 2).reshape(turns, per_turn, 2, inner_width)

    def turn_step(state, block):
        keep_block, b_block, r_block, x_block = block
        outputs = []
        for row_index in range(per_turn):
            x_float = x_block[row_index].astype(jnp.float32)
            state = (
                keep_block[row_index][:, None, None] * decay_mult[None] * state
                + drive_gain[None] * b_block[row_index][:, :, None] * x_float[:, None, :]
            )
            if want_rows:
                outputs.append(jnp.sum(r_block[row_index][:, :, None] * state, axis=1))
        if want_rows:
            return (state, jnp.stack(outputs))
        return (state, jnp.zeros((), jnp.float32))

    final_state, produced = lax.scan(
        turn_step, start_state, (keep_blocks, b_blocks, r_blocks, x_blocks)
    )
    if want_rows:
        return (final_state, produced.reshape(row_count, 2, inner_width).transpose(1, 0, 2))
    return (final_state, None)


def body(
    hidden,
    tokens,
    edit_bounds,
    norm_gain,
    base_embed,
    w_in,
    conv_w,
    conv_b,
    proj_bc,
    decay_rate,
    skip_gain,
    w_out,
):
    row_count = hidden.shape[0]
    seq_count = lax.axis_size("seq")
    where_am = lax.axis_index("seq")
    levels = seq_count.bit_length() - 1
    own_bases = lax.dynamic_slice_in_dim(tokens, where_am * row_count, row_count)
    partner_shard = hidden
    for bit_index in range(levels):
        partner_shard = from_partner(partner_shard, "seq", bit_index)
    owner_dev = seq_count - 1 - where_am
    to_gather = jnp.stack([hidden, partner_shard])
    gathered = lax.all_gather(to_gather, "ch", axis=2, tiled=True)
    normed = norm_rows(gathered[0], own_bases, norm_gain, base_embed)
    far_bases = lax.dynamic_slice_in_dim(tokens, owner_dev * row_count, row_count)
    partner = norm_rows(gathered[1], far_bases, norm_gain, base_embed)
    offsets = jnp.arange(row_count, dtype=jnp.int32)
    keep_ahead = keep_rows(where_am * row_count + offsets, edit_bounds)
    back_rows = partner[::-1, ::-1]
    keep_back = keep_rows(owner_dev * row_count + row_count - 1 - offsets, edit_bounds)
    stacked = jnp.concatenate([normed, back_rows], axis=0)
    both_proj = lax.dot_general(
        stacked, w_in, (((1,), (1,)), ((), ())), preferred_element_type=jnp.float32
    ).astype(jnp.bfloat16)
    x_part = both_proj[:, 0, :].reshape(2, row_count, -1)
    z_part = both_proj[:, 1, :].reshape(2, row_count, -1)
    rims = x_part[:, row_count - CONV + 1 :, :]
    rims_in = passed_along(rims, "seq", 1)
    padded = jnp.concatenate([rims_in, x_part], axis=1)
    conv_sum = conv_b[None, None, :] + jnp.zeros(x_part.shape, jnp.float32)
    for tap_index in range(CONV):
        conv_sum = (
            conv_sum
            + padded[:, tap_index : tap_index + row_count, :].astype(jnp.float32)
            * conv_w[tap_index][None, None, :]
        )
    mixed_in = jax.nn.silu(conv_sum).astype(jnp.bfloat16)
    partial_bc = jnp.einsum("kc,slc->skl", proj_bc, mixed_in, preferred_element_type=jnp.float32)
    inputs_bc = lax.psum(partial_bc, "ch")
    state_size = decay_rate.shape[0]
    inputs_b = inputs_bc[:, :state_size]
    inputs_r = inputs_bc[:, state_size:]
    decay_mult = jnp.exp(-decay_rate)
    drive_gain = jnp.sqrt(-jnp.expm1(-2.0 * decay_rate))
    keep_both = jnp.stack([keep_ahead, keep_back])
    zero_state = jnp.zeros((2,) + decay_rate.shape, jnp.float32)
    local_end, unused = run_chain(
        zero_state, keep_both, inputs_b, inputs_r, mixed_in, decay_mult, drive_gain, False
    )
    block_decay = jnp.exp(-float(row_count) * decay_rate)
    pass_ahead = jnp.prod(keep_ahead) * block_decay
    pass_back = jnp.prod(keep_back) * block_decay
    identity_pair = (jnp.ones_like(decay_mult), jnp.zeros_like(decay_mult))
    carried = carried_in(
        (pass_ahead, local_end[0], pass_back, local_end[1]),
        "seq",
        link_pair,
        identity_pair + identity_pair,
    )
    carry_fore = carried[1]
    carry_aft = carried[3]
    entering = jnp.stack([carry_fore, carry_aft])
    final_unused, read_rows = run_chain(
        entering, keep_both, inputs_b, inputs_r, mixed_in, decay_mult, drive_gain, True
    )
    y_out = read_rows + skip_gain[None, None, :] * mixed_in.astype(jnp.float32)
    gated = (y_out * jax.nn.silu(z_part.astype(jnp.float32))).astype(jnp.bfloat16)
    gated_ahead = gated[0]
    gated_back = gated[1]
    for bit_index in range(levels):
        gated_back = from_partner(gated_back, "seq", bit_index)
    aligned = gated_back[::-1]
    summed = (
        jnp.dot(gated_ahead, w_out, preferred_element_type=jnp.float32)
        + jnp.dot(aligned, w_out, preferred_element_type=jnp.float32)[:, ::-1]
    )
    return lax.psum_scatter(summed.astype(jnp.bfloat16), "ch", scatter_dimension=1, tiled=True)


def solution(mesh):
    placed = (
        P("seq", "ch"),
        P(),
        P(),
        P(),
        P(),
        P(None, None, "ch"),
        P(None, "ch"),
        P("ch"),
        P(None, "ch"),
        P(None, "ch"),
        P("ch"),
        P("ch", None),
    )
    return jax.shard_map(
        body, mesh=mesh, in_specs=placed, out_specs=P("seq", "ch"), check_vma=False
    )
```

profile of v0, /device:TPU:4, one launch (start us, length us, event | category | flops | bytes accessed | tf_op | source)
XLA Modules:
  0.0 528.3 jit_solution(1080955099993510452)
XLA Ops:
  12.3 3.3 collective-permute-start.2
  18.2 7.3 %collective-permute-start.3 = (bf16[128,256]{1,0:T(8,128)(2,1)S(1)}, bf16[128,256]{1,0:T(8,128)(2,1)S(1)}, u32[]{:S(2)}, u32[]{:S(2)}) collective-permute-start(bf16[128,256]{1,0:T(8,128)(2,1)S(1)} %collective-permute-done.2), channel_id=1, source_target_pairs={{0,64},{64,0},{8,72},{72,8},{16,80},{80,16},{24,88},{88,24},{32,96... | collective-permute-start | bytes 196616 | tf_op jit(solution)/shard_map/ppermute | solution.py:17
  29.2 4.2 collective-permute-done.4
  36.7 2.6 fusion.187
  42.7 36.3 %all-gather.8.cloned.1.call-done = bf16[2,128,2048]{2,1,0:T(8,128)(2,1)} async-done(((bf16[2,128,256]{2,1,0:T(8,128)(2,1)}), bf16[2,128,2048]{2,1,0:T(8,128)(2,1)}) %all-gather.8.cloned.1.call-update) | async-done | bytes 1048592 | tf_op jit(solution)/shard_map/all_gather | solution.py:126
  80.5 2.9 fusion.171
  85.3 3.6 convolution_convert_fusion
  91.0 6.5 %collective-permute-done.5 = bf16[2,3,512]{2,1,0:T(4,128)(2,1)S(1)} collective-permute-done((bf16[2,3,512]{2,1,0:T(4,128)(2,1)S(1)}, bf16[2,3,512]{2,1,0:T(4,128)(2,1)S(1)}, u32[]{:S(2)}, u32[]{:S(2)}) %collective-permute-start.5) | collective-permute-done | bytes 6176 | tf_op jit(solution)/shard_map/ppermute | solution.py:23
  98.4 34.0 %psum.7 = f32[2,32,128]{2,1,0:T(8,128)S(1)} all-reduce(f32[2,32,128]{2,1,0:T(8,128)S(1)} %convolution_bitcast_fusion), channel_id=1, replica_groups=mesh['seq'=32,'ch'=8] {'ch'}, use_global_device_ids=true, to_apply=%region_5.6 | all-reduce | flops 8192 | bytes 65536 | tf_op jit(solution)/shard_map/psum | solution.py:152
  132.5 5.1 while.41
  139.0 20.7 %all-gather.16.cloned.1.call-done = f32[512,512]{1,0:T(8,128)} async-done(((f32[16,512]{1,0:T(8,128)}), f32[512,512]{1,0:T(8,128)}) %all-gather.16.cloned.1.call-update) | async-done | bytes 1048592 | tf_op jit(solution)/shard_map/all_gather | solution.py:28
  159.7 77.5 %all-gather.14.cloned.1.call-done = f32[512,512]{1,0:T(8,128)} async-done(((f32[16,512]{1,0:T(8,128)}), f32[512,512]{1,0:T(8,128)}) %all-gather.14.cloned.1.call-update) | async-done | bytes 1048592 | tf_op jit(solution)/shard_map/all_gather | solution.py:28
  237.2 77.3 %all-gather.10.cloned.1.call-done = f32[32,16,512]{2,1,0:T(8,128)} async-done(((f32[1,16,512]{2,1,0:T(8,128)}), f32[32,16,512]{2,1,0:T(8,128)}) %all-gather.10.cloned.1.call-update) | async-done | bytes 1048592 | tf_op jit(solution)/shard_map/all_gather | solution.py:28
  314.5 77.3 %all-gather.12.cloned.1.call-done = f32[32,16,512]{2,1,0:T(8,128)} async-done(((f32[1,16,512]{2,1,0:T(8,128)}), f32[32,16,512]{2,1,0:T(8,128)}) %all-gather.12.cloned.1.call-update) | async-done | bytes 1048592 | tf_op jit(solution)/shard_map/all_gather | solution.py:28
  391.8 13.8 %while.39 = (s32[]{:T(128)}, f32[16,512]{1,0:T(8,128)S(1)}, f32[16,512]{1,0:T(8,128)S(1)}, s32[]{:T(128)}, f32[32,16,512]{2,1,0:T(8,128)}, /*index=5*/f32[32,16,...) while((s32[]{:T(128)}, f32[16,512]{1,0:T(8,128)S(1)}, ...), condition=%wide.region_10.11_spmd, body=%wide.region_9.10_spmd.sunk | while | flops 32773 | bytes 262291 | solution.py:36
  405.7 16.8 %while.40 = (s32[]{:T(128)}, f32[2,16,512]{2,1,0:T(8,128)S(1)}, f32[8,16,2,512]{3,2,1,0:T(2,128)}, f32[8,16,2]{2,1,0:T(8,128)S(1)}, f32[16,512]{1,0:T(8,128)S(1)...) while((s32[]{:T(128)}, f32[2,16,512]{2,1,0:T(8,128)S(1)}, ...), condition=%wide.region_28.29_spmd, body=%wide.region_11.28_spmd.sunk | while | flops 2818065 | bytes 1473593 | solution.py:94
  428.5 4.0 collective-permute-done.7
  432.5 6.1 %collective-permute-start.8 = (bf16[128,512]{1,0:T(8,128)(2,1)S(1)}, bf16[128,512]{1,0:T(8,128)(2,1)S(1)}, u32[]{:S(2)}, u32[]{:S(2)}) collective-permute-start(bf16[128,512]{1,0:T(8,128)(2,1)S(1)} %collective-permute-done.7), channel_id=1, source_target_pairs={{0,32},{32,0},{8,40},{40,8},{16,48},{48,16},{24,56},{56,24},{64,96... | collective-permute-start | bytes 393224 | tf_op jit(solution)/shard_map/ppermute | solution.py:17
  438.6 6.3 %collective-permute-done.8 = bf16[128,512]{1,0:T(8,128)(2,1)S(1)} collective-permute-done((bf16[128,512]{1,0:T(8,128)(2,1)S(1)}, bf16[128,512]{1,0:T(8,128)(2,1)S(1)}, u32[]{:S(2)}, u32[]{:S(2)}) %collective-permute-start.8) | collective-permute-done | bytes 131104 | tf_op jit(solution)/shard_map/ppermute | solution.py:17
  444.9 8.6 %collective-permute-start.9 = (bf16[128,512]{1,0:T(8,128)(2,1)S(1)}, bf16[128,512]{1,0:T(8,128)(2,1)S(1)}, u32[]{:S(2)}, u32[]{:S(2)}) collective-permute-start(bf16[128,512]{1,0:T(8,128)(2,1)S(1)} %collective-permute-done.8), channel_id=1, source_target_pairs={{0,64},{64,0},{8,72},{72,8},{16,80},{80,16},{24,88},{88,24},{32,96... | collective-permute-start | bytes 393224 | tf_op jit(solution)/shard_map/ppermute | solution.py:17
  453.5 4.9 collective-permute-done.9
  458.9 6.0 %collective-permute-done.10 = bf16[128,512]{1,0:T(8,128)(2,1)S(1)} collective-permute-done((bf16[128,512]{1,0:T(8,128)(2,1)S(1)}, bf16[128,512]{1,0:T(8,128)(2,1)S(1)}, u32[]{:S(2)}, u32[]{:S(2)}) %collective-permute-start.10) | collective-permute-done | bytes 131104 | tf_op jit(solution)/shard_map/ppermute | solution.py:17
  466.6 9.3 %rev.11 = f32[128,2048]{1,0:T(8,128)} reverse(f32[128,2048]{1,0:T(8,128)} %fusion.199), dimensions={1} | reverse | bytes 2097152 | tf_op jit(solution)/shard_map/rev | solution.py:188
  478.1 43.4 %reduce-scatter.2.cloned.1.call-done = bf16[128,256]{1,0:T(8,128)(2,1)} async-done(((bf16[128,2048]{1,0:T(8,128)(2,1)}), bf16[128,256]{1,0:T(8,128)(2,1)}) %reduce-scatter.2.cloned.1.call-update) | async-done | bytes 65552 | tf_op jit(solution)/shard_map/reduce_scatter | solution.py:190
  (318 shorter events, 70.9 us)
Async XLA Ops:
  6.5 451.9 %copy-start = (bf16[512,2048]{1,0:T(8,128)(2,1)S(1)}, bf16[512,2048]{1,0:T(8,128)(2,1)}, u32[]{:S(2)}) copy-start(bf16[512,2048]{1,0:T(8,128)(2,1)} %param.29) | copy-start | bytes 6291460
  6.5 72.5 %all-gather.8.cloned.1.call-start = ((), (), s32[]{:S(2)}) async-start(), calls=%async_computation.1 | async-start | bytes 1179648 | tf_op jit(solution)/shard_map/all_gather | solution.py:126
  6.5 1.5 collective-permute-start
  8.0 4.3 collective-permute-start.1
  12.3 5.8 %collective-permute-start.2 = (bf16[128,256]{1,0:T(8,128)(2,1)S(1)}, bf16[128,256]{1,0:T(8,128)(2,1)S(1)}, u32[]{:S(2)}, u32[]{:S(2)}) collective-permute-start(bf16[128,256]{1,0:T(8,128)(2,1)S(1)} %collective-permute-done.1), channel_id=1, source_target_pairs={{0,32},{32,0},{8,40},{40,8},{16,48},{48,16},{24,56},{56,24},{64,96... | collective-permute-start | bytes 196616 | tf_op jit(solution)/shard_map/ppermute | solution.py:17
  18.2 9.5 %collective-permute-start.3 = (bf16[128,256]{1,0:T(8,128)(2,1)S(1)}, bf16[128,256]{1,0:T(8,128)(2,1)S(1)}, u32[]{:S(2)}, u32[]{:S(2)}) collective-permute-start(bf16[128,256]{1,0:T(8,128)(2,1)S(1)} %collective-permute-done.2), channel_id=1, source_target_pairs={{0,64},{64,0},{8,72},{72,8},{16,80},{80,16},{24,88},{88,24},{32,96... | collective-permute-start | bytes 196616 | tf_op jit(solution)/shard_map/ppermute | solution.py:17
  27.7 5.8 %collective-permute-start.4 = (bf16[128,256]{1,0:T(8,128)(2,1)S(1)}, bf16[128,256]{1,0:T(8,128)(2,1)S(1)}, u32[]{:S(2)}, u32[]{:S(2)}) collective-permute-start(bf16[128,256]{1,0:T(8,128)(2,1)S(1)} %collective-permute-done.3), channel_id=1, source_target_pairs={{0,128},{128,0},{8,136},{136,8},{16,144},{144,16},{24,152},{152,24... | collective-permute-start | bytes 196616 | tf_op jit(solution)/shard_map/ppermute | solution.py:17
  35.0 124.7 %all-gather.16.cloned.1.call-start = ((), (), s32[]{:S(2)}) async-start(), calls=%async_computation.6 | async-start | bytes 1081344 | tf_op jit(solution)/shard_map/all_gather | solution.py:28
  39.3 197.9 %all-gather.14.cloned.1.call-start = ((), (), s32[]{:S(2)}) async-start(), calls=%async_computation.5 | async-start | bytes 1081344 | tf_op jit(solution)/shard_map/all_gather | solution.py:28
  40.1 274.4 %all-gather.10.cloned.1.call-start = ((), (), s32[]{:S(2)}) async-start(), calls=%async_computation.2 | async-start | bytes 1081344 | tf_op jit(solution)/shard_map/all_gather | solution.py:28
  85.3 12.3 %copy-start.2 = (f32[512]{0:T(512)S(1)}, f32[512]{0:T(512)}, u32[]{:S(2)}) copy-start(f32[512]{0:T(512)} %param.25) | copy-start | bytes 6148
  88.9 9.3 %copy-start.1 = (bf16[32,512]{1,0:T(8,128)(2,1)S(1)}, bf16[32,512]{1,0:T(8,128)(2,1)}, u32[]{:S(2)}) copy-start(bf16[32,512]{1,0:T(8,128)(2,1)} %param.26) | copy-start | bytes 98308
  89.0 8.6 %collective-permute-start.5 = (bf16[2,3,512]{2,1,0:T(4,128)(2,1)S(1)}, bf16[2,3,512]{2,1,0:T(4,128)(2,1)S(1)}, u32[]{:S(2)}, u32[]{:S(2)}) collective-permute-start(bf16[2,3,512]{2,1,0:T(4,128)(2,1)S(1)} %slice.623), channel_id=1, source_target_pairs={{0,8},{8,16},{16,24},{24,32},{32,40},{40,48},{48,56},{56,64},{64,7... | collective-permute-start | bytes 18440 | tf_op jit(solution)/shard_map/ppermute | solution.py:23
  138.3 253.6 %all-gather.12.cloned.1.call-start = ((), (), s32[]{:S(2)}) async-start(), calls=%async_computation.3 | async-start | bytes 1081344 | tf_op jit(solution)/shard_map/all_gather | solution.py:28
  138.9 382.6 %reduce-scatter.2.cloned.1.call-start = ((), (), s32[]{:S(2)}) async-start(), calls=%async_computation.4 | async-start | bytes 589824 | tf_op jit(solution)/shard_map/reduce_scatter | solution.py:190
  405.7 16.8 %copy-start.3 = (f32[512]{0:T(512)S(1)}, f32[512]{0:T(512)}, u32[]{:S(2)}) copy-start(f32[512]{0:T(512)} %param.28) | copy-start | bytes 6148
  423.7 2.2 collective-permute-start.6
  425.9 6.7 %collective-permute-start.7 = (bf16[128,512]{1,0:T(8,128)(2,1)S(1)}, bf16[128,512]{1,0:T(8,128)(2,1)S(1)}, u32[]{:S(2)}, u32[]{:S(2)}) collective-permute-start(bf16[128,512]{1,0:T(8,128)(2,1)S(1)} %collective-permute-done.6), channel_id=1, source_target_pairs={{0,16},{16,0},{8,24},{24,8},{32,48},{48,32},{40,56},{56,40},{64,80... | collective-permute-start | bytes 393224 | tf_op jit(solution)/shard_map/ppermute | solution.py:17
  432.5 12.4 %collective-permute-start.8 = (bf16[128,512]{1,0:T(8,128)(2,1)S(1)}, bf16[128,512]{1,0:T(8,128)(2,1)S(1)}, u32[]{:S(2)}, u32[]{:S(2)}) collective-permute-start(bf16[128,512]{1,0:T(8,128)(2,1)S(1)} %collective-permute-done.7), channel_id=1, source_target_pairs={{0,32},{32,0},{8,40},{40,8},{16,48},{48,16},{24,56},{56,24},{64,96... | collective-permute-start | bytes 393224 | tf_op jit(solution)/shard_map/ppermute | solution.py:17
  444.9 13.5 %collective-permute-start.9 = (bf16[128,512]{1,0:T(8,128)(2,1)S(1)}, bf16[128,512]{1,0:T(8,128)(2,1)S(1)}, u32[]{:S(2)}, u32[]{:S(2)}) collective-permute-start(bf16[128,512]{1,0:T(8,128)(2,1)S(1)} %collective-permute-done.8), channel_id=1, source_target_pairs={{0,64},{64,0},{8,72},{72,8},{16,80},{80,16},{24,88},{88,24},{32,96... | collective-permute-start | bytes 393224 | tf_op jit(solution)/shard_map/ppermute | solution.py:17
  458.4 6.5 %collective-permute-start.10 = (bf16[128,512]{1,0:T(8,128)(2,1)S(1)}, bf16[128,512]{1,0:T(8,128)(2,1)S(1)}, u32[]{:S(2)}, u32[]{:S(2)}) collective-permute-start(bf16[128,512]{1,0:T(8,128)(2,1)S(1)} %collective-permute-done.9), channel_id=1, source_target_pairs={{0,128},{128,0},{8,136},{136,8},{16,144},{144,16},{24,152},{152,24... | collective-permute-start | bytes 393224 | tf_op jit(solution)/shard_map/ppermute | solution.py:17
Sparse Core Ops, SparseCore 0:
  35.1 43.8 all-gather.7
  81.8 77.8 all-gather.15
  162.5 74.6 all-gather.13
  239.8 74.5 all-gather.9
  317.1 74.6 all-gather.11
  478.2 43.2 reduce-scatter.1
where the time goes:
time: 532 us; the launch traced here: 528 us
  waiting for transfers between devices  375 us (70%)
  other arithmetic  38.7 us (7%)
  starting transfers between devices  34.7 us (7%)
  blocking collectives  34 us (6%)
  local copies, waits for them, and re-layouts  24.6 us (5%)
  between operations  13.7 us (3%)
  matrix products  5.68 us (1%)
    all_gather x4, waiting for transfers between devices, carried_in(): gathered = jax.tree.map(lambda a: lax.all_gather(a, axis), part)  253 us
    reduce_scatter x1, waiting for transfers between devices, body(): lax.psum_scatter(summed.astype(jnp.bfloat16), 'ch', scatter_dimension=1,...  43.4 us
    all_gather x1, waiting for transfers between devices, body(): gathered = lax.all_gather(to_gather, 'ch', axis=2, tiled=True)  36.3 us
    ppermute x10, waiting for transfers between devices, from_partner(): return lax.ppermute(block, axis, route)  35.1 us
    psum x1, blocking collectives, body(): inputs_bc = lax.psum(partial_bc, 'ch')  34 us
    ppermute x10, starting transfers between devices, from_partner(): return lax.ppermute(block, axis, route)  32.5 us
    add x16, other arithmetic, link(): return (before[0] * follow[0], before[1] * follow[0] + follow[1])  13.5 us
  transfers between devices with their start and end apart: 17, of which 17 were waited for; matrix products, arithmetic and copies ran while one was open for 4% of the time, Pallas kernels for 0%

commit v1 on v0

--- a/solution.py
+++ b/solution.py
@@ -123,7 +123,9 @@
         partner_shard = from_partner(partner_shard, "seq", bit_index)
     owner_dev = seq_count - 1 - where_am
     to_gather = jnp.stack([hidden, partner_shard])
-    gathered = lax.all_gather(to_gather, "ch", axis=2, tiled=True)
+    gathered = jnp.concatenate(
+        lax.all_to_all(jnp.stack([to_gather] * lax.axis_size("ch")), "ch", 0, 0), axis=2
+    )
     normed = norm_rows(gathered[0], own_bases, norm_gain, base_embed)
     far_bases = lax.dynamic_slice_in_dim(tokens, owner_dev * row_count, row_count)
     partner = norm_rows(gathered[1], far_bases, norm_gain, base_embed)

time: 532 us -> 462 us (0.87)
  waiting for transfers between devices: 375 us -> 306 us
    all_gather x4, waiting for transfers between devices: 253 us -> 209 us  [carried_in(): gathered = jax.tree.map(lambda a: lax.all_gather(a, axis), part)]
    all_gather x1 -> x0, waiting for transfers between devices: 36.3 us -> none  [body(): gathered = lax.all_gather(to_gather, 'ch', axis=2, tiled=True)]
    all_to_all x0 -> x1, waiting for transfers between devices: none -> 12.2 us  [body(): lax.all_to_all(jnp.stack([to_gather] * lax.axis_size('ch')), 'ch', 0, 0)]
  transfers between devices with their start and end apart: 17 -> 17, of which waited for: 17 -> 16; matrix products, arithmetic and copies ran while one was open for 4% -> 4% of each run, Pallas kernels for 0% -> 0%
where the time goes in v1:
time: 462 us; the launch traced here: 459 us
  waiting for transfers between devices  306 us (66%)
  starting transfers between devices  39.9 us (9%)
  other arithmetic  35.9 us (8%)
  blocking collectives  31.5 us (7%)
  local copies, waits for them, and re-layouts  24.8 us (5%)
  between operations  13.4 us (3%)
  matrix products  5.79 us (1%)
    all_gather x4, waiting for transfers between devices, carried_in(): gathered = jax.tree.map(lambda a: lax.all_gather(a, axis), part)  209 us
    reduce_scatter x1, waiting for transfers between devices, body(): lax.psum_scatter(summed.astype(jnp.bfloat16), 'ch', scatter_dimension=1,...  43.4 us
    ppermute x10, waiting for transfers between devices, from_partner(): return lax.ppermute(block, axis, route)  34.3 us
    ppermute x10, starting transfers between devices, from_partner(): return lax.ppermute(block, axis, route)  32.7 us
    psum x1, blocking collectives, body(): inputs_bc = lax.psum(partial_bc, 'ch')  31.5 us
    add x16, other arithmetic, link(): return (before[0] * follow[0], before[1] * follow[0] + follow[1])  13.5 us
    all_to_all x1, waiting for transfers between devices, body(): lax.all_to_all(jnp.stack([to_gather] * lax.axis_size('ch')), 'ch', 0, 0)  12.2 us
    rev x1, local copies, waits for them, and re-layouts, body(): jnp.dot(aligned, w_out, preferred_element_type=jnp.float32)[:, ::-1]  9.34 us
  transfers between devices with their start and end apart: 17, of which 16 were waited for; matrix products, arithmetic and copies ran while one was open for 4% of the time, Pallas kernels for 0%

profile of v1, /device:TPU:4, one launch (start us, length us, event | category | flops | bytes accessed | tf_op | source)
XLA Modules:
  0.0 458.5 jit_solution(10507194416049495411)
XLA Ops:
  8.4 2.6 fusion.179
  16.9 3.3 collective-permute-start.2
  22.8 7.3 %collective-permute-start.3 = (bf16[128,256]{1,0:T(8,128)(2,1)S(1)}, bf16[128,256]{1,0:T(8,128)(2,1)S(1)}, u32[]{:S(2)}, u32[]{:S(2)}) collective-permute-start(bf16[128,256]{1,0:T(8,128)(2,1)S(1)} %collective-permute-done.2), channel_id=1, source_target_pairs={{0,64},{64,0},{8,72},{72,8},{16,80},{80,16},{24,88},{88,24},{32,96... | collective-permute-start | bytes 196616 | tf_op jit(solution)/shard_map/ppermute | solution.py:17
  33.9 4.2 collective-permute-done.4
  40.0 5.1 %all-to-all-start = ((bf16[8,2,128,256]{3,2,1,0:T(8,128)(2,1)}), bf16[8,2,128,256]{3,2,1,0:T(8,128)(2,1)S(1)}, u32[]{:S(2)}, u32[]{:S(2)}) async-start(bf16[8,2,128,256]{3,2,1,0:T(8,128)(2,1)} %stack.89), calls=%async_computation | async-start | bytes 2097152 | tf_op jit(solution)/shard_map/all_to_all | solution.py:127
  45.3 12.2 %all-to-all-done = bf16[8,2,128,256]{3,2,1,0:T(8,128)(2,1)S(1)} async-done(((bf16[8,2,128,256]{3,2,1,0:T(8,128)(2,1)}), bf16[8,2,128,256]{3,2,1,0:T(8,128)(2,1)S(1)}, u32[]{:S(2)}, u32[]{:S(2)}) %all-to-all-start) | async-done | bytes 1048608 | tf_op jit(solution)/shard_map/all_to_all | solution.py:127
  62.2 3.7 convolution_convert_fusion
  68.0 6.5 %collective-permute-done.5 = bf16[2,3,512]{2,1,0:T(4,128)(2,1)S(1)} collective-permute-done((bf16[2,3,512]{2,1,0:T(4,128)(2,1)S(1)}, bf16[2,3,512]{2,1,0:T(4,128)(2,1)S(1)}, u32[]{:S(2)}, u32[]{:S(2)}) %collective-permute-start.5) | collective-permute-done | bytes 6176 | tf_op jit(solution)/shard_map/ppermute | solution.py:23
  75.4 31.5 %psum.7 = f32[2,32,128]{2,1,0:T(8,128)S(1)} all-reduce(f32[2,32,128]{2,1,0:T(8,128)S(1)} %convolution_bitcast_fusion), channel_id=1, replica_groups=mesh['seq'=32,'ch'=8] {'ch'}, use_global_device_ids=true, to_apply=%region_5.6 | all-reduce | flops 8192 | bytes 65536 | tf_op jit(solution)/shard_map/psum | solution.py:154
  107.1 5.1 %while.41 = (s32[]{:T(128)}, f32[2,16,512]{2,1,0:T(8,128)S(1)}, f32[8,16,2]{2,1,0:T(8,128)S(1)}, f32[16,512]{1,0:T(8,128)S(1)}, f32[16,512]{1,0:T(8,128)S(1)}, /...) while((s32[]{:T(128)}, f32[2,16,512]{2,1,0:T(8,128)S(1)}, ...), condition=%wide.region_7.8_spmd.clone, body=%wide.region_6.7_spmd.clone.sunk | while | flops 1343506 | bytes 367571 | solution.py:94
  113.6 53.9 %all-gather.11.cloned.1.call-done = f32[512,512]{1,0:T(8,128)} async-done(((f32[16,512]{1,0:T(8,128)}), f32[512,512]{1,0:T(8,128)}) %all-gather.11.cloned.1.call-update) | async-done | bytes 1048592 | tf_op jit(solution)/shard_map/all_gather | solution.py:28
  167.5 77.4 %all-gather.7.cloned.1.call-done = f32[32,16,512]{2,1,0:T(8,128)} async-done(((f32[1,16,512]{2,1,0:T(8,128)}), f32[32,16,512]{2,1,0:T(8,128)}) %all-gather.7.cloned.1.call-update) | async-done | bytes 1048592 | tf_op jit(solution)/shard_map/all_gather | solution.py:28
  245.0 77.4 %all-gather.9.cloned.1.call-done = f32[32,16,512]{2,1,0:T(8,128)} async-done(((f32[1,16,512]{2,1,0:T(8,128)}), f32[32,16,512]{2,1,0:T(8,128)}) %all-gather.9.cloned.1.call-update) | async-done | bytes 1048592 | tf_op jit(solution)/shard_map/all_gather | solution.py:28
  322.3 13.8 %while.39 = (s32[]{:T(128)}, f32[16,512]{1,0:T(8,128)S(1)}, f32[16,512]{1,0:T(8,128)S(1)}, s32[]{:T(128)}, f32[32,16,512]{2,1,0:T(8,128)}, /*index=5*/f32[32,16,...) while((s32[]{:T(128)}, f32[16,512]{1,0:T(8,128)S(1)}, ...), condition=%wide.region_10.11_spmd, body=%wide.region_9.10_spmd.sunk | while | flops 32773 | bytes 262291 | solution.py:36
  336.2 16.8 %while.40 = (s32[]{:T(128)}, f32[2,16,512]{2,1,0:T(8,128)S(1)}, f32[8,16,2,512]{3,2,1,0:T(2,128)}, f32[8,16,2]{2,1,0:T(8,128)S(1)}, f32[16,512]{1,0:T(8,128)S(1)...) while((s32[]{:T(128)}, f32[2,16,512]{2,1,0:T(8,128)S(1)}, ...), condition=%wide.region_28.29_spmd, body=%wide.region_11.28_spmd.sunk | while | flops 2818065 | bytes 1473593 | solution.py:94
  356.4 2.6 collective-permute-start.7
  359.0 4.0 collective-permute-done.7
  363.0 6.1 %collective-permute-start.8 = (bf16[128,512]{1,0:T(8,128)(2,1)S(1)}, bf16[128,512]{1,0:T(8,128)(2,1)S(1)}, u32[]{:S(2)}, u32[]{:S(2)}) collective-permute-start(bf16[128,512]{1,0:T(8,128)(2,1)S(1)} %collective-permute-done.7), channel_id=1, source_target_pairs={{0,32},{32,0},{8,40},{40,8},{16,48},{48,16},{24,56},{56,24},{64,96... | collective-permute-start | bytes 393224 | tf_op jit(solution)/shard_map/ppermute | solution.py:17
  369.1 6.3 %collective-permute-done.8 = bf16[128,512]{1,0:T(8,128)(2,1)S(1)} collective-permute-done((bf16[128,512]{1,0:T(8,128)(2,1)S(1)}, bf16[128,512]{1,0:T(8,128)(2,1)S(1)}, u32[]{:S(2)}, u32[]{:S(2)}) %collective-permute-start.8) | collective-permute-done | bytes 131104 | tf_op jit(solution)/shard_map/ppermute | solution.py:17
  375.4 8.6 %collective-permute-start.9 = (bf16[128,512]{1,0:T(8,128)(2,1)S(1)}, bf16[128,512]{1,0:T(8,128)(2,1)S(1)}, u32[]{:S(2)}, u32[]{:S(2)}) collective-permute-start(bf16[128,512]{1,0:T(8,128)(2,1)S(1)} %collective-permute-done.8), channel_id=1, source_target_pairs={{0,64},{64,0},{8,72},{72,8},{16,80},{80,16},{24,88},{88,24},{32,96... | collective-permute-start | bytes 393224 | tf_op jit(solution)/shard_map/ppermute | solution.py:17
  384.0 4.9 %collective-permute-done.9 = bf16[128,512]{1,0:T(8,128)(2,1)S(1)} collective-permute-done((bf16[128,512]{1,0:T(8,128)(2,1)S(1)}, bf16[128,512]{1,0:T(8,128)(2,1)S(1)}, u32[]{:S(2)}, u32[]{:S(2)}) %collective-permute-start.9) | collective-permute-done | bytes 131104 | tf_op jit(solution)/shard_map/ppermute | solution.py:17
  389.4 6.0 %collective-permute-done.10 = bf16[128,512]{1,0:T(8,128)(2,1)S(1)} collective-permute-done((bf16[128,512]{1,0:T(8,128)(2,1)S(1)}, bf16[128,512]{1,0:T(8,128)(2,1)S(1)}, u32[]{:S(2)}, u32[]{:S(2)}) %collective-permute-start.10) | collective-permute-done | bytes 131104 | tf_op jit(solution)/shard_map/ppermute | solution.py:17
  397.0 9.3 %rev.11 = f32[128,2048]{1,0:T(8,128)} reverse(f32[128,2048]{1,0:T(8,128)} %fusion.191), dimensions={1} | reverse | bytes 2097152 | tf_op jit(solution)/shard_map/rev | solution.py:190
  408.6 43.4 %reduce-scatter.2.cloned.1.call-done = bf16[128,256]{1,0:T(8,128)(2,1)} async-done(((bf16[128,2048]{1,0:T(8,128)(2,1)}), bf16[128,256]{1,0:T(8,128)(2,1)}) %reduce-scatter.2.cloned.1.call-update) | async-done | bytes 65552 | tf_op jit(solution)/shard_map/reduce_scatter | solution.py:192
  (327 shorter events, 67.1 us)
Async XLA Ops:
  6.5 382.4 %copy-start = (bf16[512,2048]{1,0:T(8,128)(2,1)S(1)}, bf16[512,2048]{1,0:T(8,128)(2,1)}, u32[]{:S(2)}) copy-start(bf16[512,2048]{1,0:T(8,128)(2,1)} %param.29) | copy-start | bytes 6291460
  6.5 38.7 %copy-start.4 = (f32[4,512]{1,0:T(4,128)S(1)}, f32[4,512]{1,0:T(4,128)}, u32[]{:S(2)}) copy-start(f32[4,512]{1,0:T(4,128)} %param.24) | copy-start | bytes 24580
  6.5 38.7 %copy-start.2 = (f32[4,2048]{1,0:T(4,128)S(1)}, f32[4,2048]{1,0:T(4,128)}, u32[]{:S(2)}) copy-start(f32[4,2048]{1,0:T(4,128)} %param.22) | copy-start | bytes 98308
  6.5 107.1 %all-gather.13.cloned.1.call-start = ((), (), s32[]{:S(2)}) async-start(), calls=%async_computation.6 | async-start | bytes 1081344 | tf_op jit(solution)/shard_map/all_gather | solution.py:28
  11.0 156.5 %all-gather.11.cloned.1.call-start = ((), (), s32[]{:S(2)}) async-start(), calls=%async_computation.5 | async-start | bytes 1081344 | tf_op jit(solution)/shard_map/all_gather | solution.py:28
  11.1 1.6 collective-permute-start
  12.6 4.3 collective-permute-start.1
  16.9 5.8 %collective-permute-start.2 = (bf16[128,256]{1,0:T(8,128)(2,1)S(1)}, bf16[128,256]{1,0:T(8,128)(2,1)S(1)}, u32[]{:S(2)}, u32[]{:S(2)}) collective-permute-start(bf16[128,256]{1,0:T(8,128)(2,1)S(1)} %collective-permute-done.1), channel_id=1, source_target_pairs={{0,32},{32,0},{8,40},{40,8},{16,48},{48,16},{24,56},{56,24},{64,96... | collective-permute-start | bytes 196616 | tf_op jit(solution)/shard_map/ppermute | solution.py:17
  22.8 9.6 %collective-permute-start.3 = (bf16[128,256]{1,0:T(8,128)(2,1)S(1)}, bf16[128,256]{1,0:T(8,128)(2,1)S(1)}, u32[]{:S(2)}, u32[]{:S(2)}) collective-permute-start(bf16[128,256]{1,0:T(8,128)(2,1)S(1)} %collective-permute-done.2), channel_id=1, source_target_pairs={{0,64},{64,0},{8,72},{72,8},{16,80},{80,16},{24,88},{88,24},{32,96... | collective-permute-start | bytes 196616 | tf_op jit(solution)/shard_map/ppermute | solution.py:17
  32.3 5.8 %collective-permute-start.4 = (bf16[128,256]{1,0:T(8,128)(2,1)S(1)}, bf16[128,256]{1,0:T(8,128)(2,1)S(1)}, u32[]{:S(2)}, u32[]{:S(2)}) collective-permute-start(bf16[128,256]{1,0:T(8,128)(2,1)S(1)} %collective-permute-done.3), channel_id=1, source_target_pairs={{0,128},{128,0},{8,136},{136,8},{16,144},{144,16},{24,152},{152,24... | collective-permute-start | bytes 196616 | tf_op jit(solution)/shard_map/ppermute | solution.py:17
  40.0 17.4 %all-to-all-start = ((bf16[8,2,128,256]{3,2,1,0:T(8,128)(2,1)}), bf16[8,2,128,256]{3,2,1,0:T(8,128)(2,1)S(1)}, u32[]{:S(2)}, u32[]{:S(2)}) async-start(bf16[8,2,128,256]{3,2,1,0:T(8,128)(2,1)} %stack.89), calls=%async_computation | async-start | bytes 2097152 | tf_op jit(solution)/shard_map/all_to_all | solution.py:127
  45.2 199.8 %all-gather.7.cloned.1.call-start = ((), (), s32[]{:S(2)}) async-start(), calls=%async_computation.2 | async-start | bytes 1081344 | tf_op jit(solution)/shard_map/all_gather | solution.py:28
  58.0 0.7 copy-start.3
  62.2 12.4 %copy-start.5 = (f32[512]{0:T(512)S(1)}, f32[512]{0:T(512)}, u32[]{:S(2)}) copy-start(f32[512]{0:T(512)} %param.25) | copy-start | bytes 6148
  65.9 9.3 %copy-start.1 = (bf16[32,512]{1,0:T(8,128)(2,1)S(1)}, bf16[32,512]{1,0:T(8,128)(2,1)}, u32[]{:S(2)}) copy-start(bf16[32,512]{1,0:T(8,128)(2,1)} %param.26) | copy-start | bytes 98308
  66.0 8.6 %collective-permute-start.5 = (bf16[2,3,512]{2,1,0:T(4,128)(2,1)S(1)}, bf16[2,3,512]{2,1,0:T(4,128)(2,1)S(1)}, u32[]{:S(2)}, u32[]{:S(2)}) collective-permute-start(bf16[2,3,512]{2,1,0:T(4,128)(2,1)S(1)} %slice.625), channel_id=1, source_target_pairs={{0,8},{8,16},{16,24},{24,32},{32,40},{40,48},{48,56},{56,64},{64,7... | collective-permute-start | bytes 18440 | tf_op jit(solution)/shard_map/ppermute | solution.py:23
  112.8 209.5 %all-gather.9.cloned.1.call-start = ((), (), s32[]{:S(2)}) async-start(), calls=%async_computation.3 | async-start | bytes 1081344 | tf_op jit(solution)/shard_map/all_gather | solution.py:28
  113.4 338.5 %reduce-scatter.2.cloned.1.call-start = ((), (), s32[]{:S(2)}) async-start(), calls=%async_computation.4 | async-start | bytes 589824 | tf_op jit(solution)/shard_map/reduce_scatter | solution.py:192
  336.2 16.8 %copy-start.6 = (f32[512]{0:T(512)S(1)}, f32[512]{0:T(512)}, u32[]{:S(2)}) copy-start(f32[512]{0:T(512)} %param.28) | copy-start | bytes 6148
  354.2 2.2 collective-permute-start.6
  356.4 6.7 %collective-permute-start.7 = (bf16[128,512]{1,0:T(8,128)(2,1)S(1)}, bf16[128,512]{1,0:T(8,128)(2,1)S(1)}, u32[]{:S(2)}, u32[]{:S(2)}) collective-permute-start(bf16[128,512]{1,0:T(8,128)(2,1)S(1)} %collective-permute-done.6), channel_id=1, source_target_pairs={{0,16},{16,0},{8,24},{24,8},{32,48},{48,32},{40,56},{56,40},{64,80... | collective-permute-start | bytes 393224 | tf_op jit(solution)/shard_map/ppermute | solution.py:17
  363.0 12.4 %collective-permute-start.8 = (bf16[128,512]{1,0:T(8,128)(2,1)S(1)}, bf16[128,512]{1,0:T(8,128)(2,1)S(1)}, u32[]{:S(2)}, u32[]{:S(2)}) collective-permute-start(bf16[128,512]{1,0:T(8,128)(2,1)S(1)} %collective-permute-done.7), channel_id=1, source_target_pairs={{0,32},{32,0},{8,40},{40,8},{16,48},{48,16},{24,56},{56,24},{64,96... | collective-permute-start | bytes 393224 | tf_op jit(solution)/shard_map/ppermute | solution.py:17
  375.4 13.5 %collective-permute-start.9 = (bf16[128,512]{1,0:T(8,128)(2,1)S(1)}, bf16[128,512]{1,0:T(8,128)(2,1)S(1)}, u32[]{:S(2)}, u32[]{:S(2)}) collective-permute-start(bf16[128,512]{1,0:T(8,128)(2,1)S(1)} %collective-permute-done.8), channel_id=1, source_target_pairs={{0,64},{64,0},{8,72},{72,8},{16,80},{80,16},{24,88},{88,24},{32,96... | collective-permute-start | bytes 393224 | tf_op jit(solution)/shard_map/ppermute | solution.py:17
  388.9 6.5 %collective-permute-start.10 = (bf16[128,512]{1,0:T(8,128)(2,1)S(1)}, bf16[128,512]{1,0:T(8,128)(2,1)S(1)}, u32[]{:S(2)}, u32[]{:S(2)}) collective-permute-start(bf16[128,512]{1,0:T(8,128)(2,1)S(1)} %collective-permute-done.9), channel_id=1, source_target_pairs={{0,128},{128,0},{8,136},{136,8},{16,144},{144,16},{24,152},{152,24... | collective-permute-start | bytes 393224 | tf_op jit(solution)/shard_map/ppermute | solution.py:17
Sparse Core Ops, SparseCore 0:
  11.1 78.9 all-gather.12
  92.9 74.6 all-gather.10
  170.3 74.5 all-gather.6
  247.6 74.6 all-gather.8
  408.7 43.2 reduce-scatter.1
